TPU v7x, 32 devices: a whole 2x2x4 slice. The times are simulated.
32 devices in a mesh: freq: 4 (over z), pts: 8 (over y, x, core).
Axes of the slice: x: 2, y: 2, z: 4, core: 2. Of those that a mesh axis runs over, the one named last changes fastest.
Arguments:
- histories: float32 [8, 2048, 4096], P(None, ('freq', 'pts')), may hold values from -6 to 6
- point_weight: float32 [4096], P('pts'), may hold values from 0.5 to 2
- basis: float32 [4096, 4096], P('pts', 'freq'), may hold values from -0.09375 to 0.09375
Outputs:
- coeffs: float32 [8, 2, 256, 4096], P(None, None, 'freq', 'pts')
All inputs are finite; a program needn't handle non-finite values.
Results may differ from a plain program's by a relative error of at most 0.00011.
Values sent between devices are 32-bit elements; how exact they have to be, the bound alone decides.
A program may use at most 128 MiB of HBM per device.

v0:
```python
import jax
import jax.numpy as jnp
from jax import lax
from jax.sharding import PartitionSpec as P

F = 256


def make_table(times, total, bins):
    freqs = jnp.arange(1, bins + 1, dtype=jnp.int32)
    phase_int = times[:, None] * freqs[None, :] % total
    angle = 2.0 * jnp.pi / total * phase_int.astype(jnp.float32)
    window = 0.5 - 0.5 * jnp.cos(2.0 * jnp.pi / total * times.astype(jnp.float32))
    scale = (window / jnp.sqrt(jnp.float32(total)))[:, None]
    return jnp.concatenate([jnp.cos(angle) * scale, -jnp.sin(angle) * scale], axis=1)


def local(histories, point_weight, basis):
    freq_count = lax.axis_size("freq")
    pts_count = lax.axis_size("pts")
    cases, time_local, all_points = histories.shape
    pts_local = all_points // (freq_count * pts_count)
    shaped = histories.reshape(cases, time_local, pts_count, freq_count, pts_local)
    moved = lax.all_to_all(
        lax.all_to_all(shaped, "freq", split_axis=3, concat_axis=1, tiled=True),
        "pts",
        split_axis=2,
        concat_axis=1,
        tiled=True,
    )
    series = moved.reshape(cases, time_local * freq_count * pts_count, pts_local)
    total_time = series.shape[1]
    position = jnp.arange(total_time, dtype=jnp.int32)
    block_index = position // time_local
    sender_pts = block_index // freq_count
    sender_freq = block_index % freq_count
    times = (sender_freq * pts_count + sender_pts) * time_local + position % time_local
    table = make_table(times, total_time, F)
    spectrum = jnp.einsum("stp,tk->skp", series, table, precision=lax.Precision.HIGHEST)
    spectrum = spectrum.reshape(cases, 2, F, pts_local)
    harmonics = basis.shape[1] * freq_count
    swapped = lax.all_to_all(spectrum, "freq", split_axis=2, concat_axis=3, tiled=True)
    bins_local = swapped.shape[2]
    weighted = (swapped * point_weight[None, None, None, :]).reshape(
        cases * 2 * bins_local, swapped.shape[3]
    )
    partial_value = jnp.dot(
        weighted,
        lax.all_gather(basis, "freq", axis=1, tiled=True),
        precision=lax.Precision.HIGHEST,
        preferred_element_type=jnp.float32,
    )
    partial_value = partial_value.reshape(cases, 2, bins_local, harmonics)
    coeffs = lax.psum_scatter(partial_value, "pts", scatter_dimension=3, tiled=True)
    return coeffs


def solution(mesh):
    return jax.shard_map(
        local,
        mesh=mesh,
        in_specs=(P(None, ("freq", "pts"), None), P("pts"), P("pts", "freq")),
        out_specs=P(None, None, "freq", "pts"),
        check_vma=False,
    )
```

profile of v0, /device:TPU:0, one launch (start us, length us, event | category | flops | bytes accessed | tf_op | source)
XLA Modules:
  0.0 684.9 jit_solution(1634910731857510469)
XLA Ops:
  6.5 10.8 %reshape.83 = f32[8,64,8,4,128]{4,3,2,1,0:T(4,128)} reshape(f32[8,64,4096]{2,1,0:T(8,128)} %param.3) | data formatting | bytes 16777216 | tf_op jit(solution)/shard_map/reshape | solution.py:23
  17.3 7.7 %copy.9 = f32[8,64,8,4,128]{4,2,1,0,3:T(8,128)} copy(f32[8,64,8,4,128]{4,3,2,1,0:T(4,128)} %reshape.83) | data formatting | bytes 16777216 | tf_op jit(solution)/shard_map/reshape | solution.py:23
  25.0 6.3 all-to-all-start
  31.3 0.0 all-gather.2.cloned.1.call-start
  31.3 0.7 all-gather.2.cloned.1.call-update
  32.0 318.2 %all-to-all-done = f32[8,64,8,4,128]{4,2,1,0,3:T(8,128)} async-done(((f32[8,64,8,4,128]{4,2,1,0,3:T(8,128)}), f32[8,64,8,4,128]{4,2,1,0,3:T(8,128)}, u32[]{:S(2)}, u32[]{:S(2)}) %all-to-all-start) | async-done | bytes 8388640 | tf_op jit(solution)/shard_map/all_to_all | solution.py:25
  350.2 3.9 copy.10
  354.2 4.8 copy.11
  358.9 4.9 all-to-all-start.1
  363.9 0.0 reduce-scatter.2.cloned.1.call-start
  364.0 0.1 subtract_multiply_fusion
  364.0 9.5 %cosine_multiply_fusion = (f32[2048,256]{0,1:T(8,128)S(1)}, f32[2048,256]{0,1:T(8,128)}) fusion(f32[2048]{0:T(1024)S(1)} %subtract_multiply_fusion, s32[256]{0:T(256)S(1)} %iota_add_fusion, s32[2048]{0:T(1024)S(1)} %fusion.19), kind=kLoop, calls=%fused_computation.16 | loop fusion | flops 8912896 | bytes 4211712 | tf_op jit(solution)/shard_map/mul | solution.py:15
  373.5 84.4 %all-to-all-done.1 = f32[8,256,8,1,128]{4,1,0,3,2:T(8,128)} async-done(((f32[8,256,8,1,128]{4,1,0,3,2:T(8,128)}), f32[8,256,8,1,128]{4,1,0,3,2:T(8,128)}, u32[]{:S(2)}, u32[]{:S(2)}) %all-to-all-start.1) | async-done | bytes 8388640 | tf_op jit(solution)/shard_map/all_to_all | solution.py:24
  457.9 0.0 copy-start
  457.9 4.1 copy.12
  462.0 0.0 copy-done
  462.0 13.9 %fusion.2 = f32[512,8,128]{2,0,1:T(8,128)S(1)} fusion(f32[8,2048,128]{2,1,0:T(8,128)S(1)} %bitcast.25, f32[2048,256]{0,1:T(8,128)S(1)} %copy-done, f32[2048,256]{0,1:T(8,128)S(1)} %get-tuple-element.5), kind=kOutput, calls=%fused_computation.3 | convolution fusion | flops 12885950464 | bytes 14680064 | tf_op jit(solution)/shard_map/stp,tk->skp/dot_general | solution.py:39
  475.9 1.6 copy.13
  477.6 48.0 %all_to_all.51 = f32[8,2,256,128]{3,1,0,2:T(2,128)S(1)} all-to-all(f32[8,2,256,128]{3,1,0,2:T(2,128)S(1)} %copy.13), channel_id=1, replica_groups=mesh['freq'=4,'pts'=8] {'freq'}, dimensions={2} | all-to-all | bytes 4194304 | tf_op jit(solution)/shard_map/all_to_all | solution.py:42
  525.6 2.7 copy.14
  528.2 0.0 copy-start.1
  528.2 2.1 all_to_all.47
  530.3 0.0 all-gather.2.cloned.1.call-done
  530.4 0.0 copy-done.1
  530.4 31.1 %fusion = f32[8,2,64,4096]{3,2,1,0:T(8,128)} fusion(f32[512,4096]{1,0:T(8,128)} %all-gather.2.cloned.1.call-done, f32[8,2,64,512]{3,2,1,0:T(8,128)S(1)} %all_to_all.47, f32[512]{0:T(512)S(1)} %copy-done.1), kind=kOutput, calls=%fused_computation | convolution fusion | flops 25770328064 | bytes 27265024 | tf_op jit(solution)/shard_map/dot_general | solution.py:47
  561.5 0.0 reduce-scatter.2.cloned.1.call-update
  561.6 116.5 %reduce-scatter.2.cloned.1.call-done = f32[8,2,64,512]{3,2,1,0:T(8,128)} async-done(((f32[8,2,64,4096]{3,2,1,0:T(8,128)}), f32[8,2,64,512]{3,2,1,0:T(8,128)}) %reduce-scatter.2.cloned.1.call-update) | async-done | bytes 2097168 | tf_op jit(solution)/shard_map/reduce_scatter | solution.py:54
  (2 shorter events, 0.0 us)
Async XLA Ops:
  25.0 325.3 %all-to-all-start = ((f32[8,64,8,4,128]{4,2,1,0,3:T(8,128)}), f32[8,64,8,4,128]{4,2,1,0,3:T(8,128)}, u32[]{:S(2)}, u32[]{:S(2)}) async-start(f32[8,64,8,4,128]{4,2,1,0,3:T(8,128)} %copy.9), calls=%async_computation | async-start | bytes 16777216 | tf_op jit(solution)/shard_map/all_to_all | solution.py:25
  31.3 499.0 %all-gather.2.cloned.1.call-start = ((), (), s32[]{:S(2)}) async-start(), calls=%async_computation.4 | async-start | bytes 10485760 | tf_op jit(solution)/shard_map/all_gather | solution.py:49
  358.9 99.0 %all-to-all-start.1 = ((f32[8,256,8,1,128]{4,1,0,3,2:T(8,128)}), f32[8,256,8,1,128]{4,1,0,3,2:T(8,128)}, u32[]{:S(2)}, u32[]{:S(2)}) async-start(f32[8,256,8,1,128]{4,1,0,3,2:T(8,128)} %copy.11), calls=%async_computation.1 | async-start | bytes 16777216 | tf_op jit(solution)/shard_map/all_to_all | solution.py:24
  363.9 314.1 %reduce-scatter.2.cloned.1.call-start = ((), (), s32[]{:S(2)}) async-start(), calls=%async_computation.5 | async-start | bytes 18874368 | tf_op jit(solution)/shard_map/reduce_scatter | solution.py:54
  457.9 4.1 copy-start
  528.2 2.1 copy-start.1
Sparse Core Ops, SparseCore 0:
  33.7 295.3 all-gather.1
  561.7 116.3 reduce-scatter.1
where the time goes:
time: 685 us
  waiting for transfers between devices  520 us (76%)
  blocking collectives  48 us (7%)
  matrix products  45.1 us (7%)
  local copies, waits for them, and re-layouts  37.6 us (5%)
  between operations  13.5 us (2%)
  starting transfers between devices  11.3 us (2%)
  other arithmetic  9.57 us (1%)
    all_to_all x1, waiting for transfers between devices, local(): lax.all_to_all(shaped, 'freq', split_axis=3, concat_axis=1, tiled=True)  318 us
    reduce_scatter x1, waiting for transfers between devices, local(): lax.psum_scatter(partial_value, 'pts', scatter_dimension=3, tiled=True)  116 us
    all_to_all x1, waiting for transfers between devices, local(): lax.all_to_all(lax.all_to_all(shaped, 'freq', split_axis=3, concat_axis=1...  84.4 us
    all_to_all x1, blocking collectives, local(): lax.all_to_all(spectrum, 'freq', split_axis=2, concat_axis=3, tiled=True)  48 us
    dot_general x1, matrix products, local(): jnp.dot(weighted, lax.all_gather(basis, 'freq', axis=1, tiled=True), prec...  31.1 us
    reshape x2, local copies, waits for them, and re-layouts, local(): histories.reshape(cases, time_local, pts_count, freq_count, pts_local)  18.4 us
    dot_general x1, matrix products, local(): jnp.einsum('stp,tk->skp', series, table, precision=lax.Precision.HIGHEST)  13.9 us
  transfers between devices with their start and end apart: 4, of which 3 were waited for; matrix products, arithmetic and copies ran while one was open for 6% of the time, Pallas kernels for 0%

commit v1 on v0

v1 whole, which is shorter than its diff:
```python
import jax
import jax.numpy as jnp
from jax import lax
from jax.sharding import PartitionSpec as P

F = 256


def make_table(times, total, bins):
    freqs = jnp.arange(1, bins + 1, dtype=jnp.int32)
    phase_int = times[:, None] * freqs[None, :] % total
    angle = 2.0 * jnp.pi / total * phase_int.astype(jnp.float32)
    window = 0.5 - 0.5 * jnp.cos(2.0 * jnp.pi / total * times.astype(jnp.float32))
    scale = (window / jnp.sqrt(jnp.float32(total)))[:, None]
    return jnp.concatenate([jnp.cos(angle) * scale, -jnp.sin(angle) * scale], axis=1)


def local(histories, point_weight, basis):
    freq_count = lax.axis_size("freq")
    pts_count = lax.axis_size("pts")
    cases, time_local, all_points = histories.shape
    pts_local = all_points // pts_count
    series = lax.all_to_all(histories, "pts", split_axis=2, concat_axis=1, tiled=True)
    plane_time = time_local * pts_count
    times = lax.axis_index("freq") * plane_time + jnp.arange(plane_time, dtype=jnp.int32)
    table = make_table(times, plane_time * freq_count, F)
    spectrum = jnp.einsum("stp,tk->skp", series, table, precision=lax.Precision.HIGH)
    spectrum = spectrum.reshape(cases, 2, F, pts_local)
    spectrum = lax.psum_scatter(spectrum, "freq", scatter_dimension=2, tiled=True)
    bins_local = spectrum.shape[2]
    harmonics = basis.shape[1] * freq_count
    weighted = (spectrum * point_weight).reshape(cases * 2 * bins_local, pts_local)
    full = lax.all_gather(basis, "freq", axis=1, tiled=True)
    partial_value = jnp.dot(
        weighted, full, precision=lax.Precision.HIGH, preferred_element_type=jnp.float32
    )
    partial_value = partial_value.reshape(cases, 2, bins_local, harmonics)
    return lax.psum_scatter(partial_value, "pts", scatter_dimension=3, tiled=True)


def solution(mesh):
    return jax.shard_map(
        local,
        mesh=mesh,
        in_specs=(P(None, ("freq", "pts"), None), P("pts"), P("pts", "freq")),
        out_specs=P(None, None, "freq", "pts"),
        check_vma=False,
    )
```

time: 685 us -> 490 us (0.72)
  waiting for transfers between devices: 520 us -> 355 us
  blocking collectives: 48 us -> 0 us
  local copies, waits for them, and re-layouts: 37.6 us -> 57.1 us
  other arithmetic: 9.57 us -> 28.5 us
  matrix products: 45.1 us -> 31.1 us
    all_to_all x2 -> x1, waiting for transfers between devices: 403 us -> 92.3 us  [local(): lax.all_to_all(histories, 'pts', split_axis=2, concat_axis=1, tiled=True)]
    reduce_scatter x0 -> x1, waiting for transfers between devices: none -> 145 us  [local(): lax.psum_scatter(spectrum, 'freq', scatter_dimension=2, tiled=True)]
    all_to_all x1 -> x0, blocking collectives: 48 us -> none  [local(): lax.all_to_all(spectrum, 'freq', split_axis=2, concat_axis=3, tiled=True)]
    unnamed x4 -> x5, local copies, waits for them, and re-layouts: 0.01 us -> 43.8 us
    all_to_all x0 -> x1, other arithmetic: none -> 26.2 us  [local(): lax.all_to_all(histories, 'pts', split_axis=2, concat_axis=1, tiled=True)]
    reshape x3 -> x0, local copies, waits for them, and re-layouts: 20.1 us -> none  [the longest x2 18.4 us: local(): histories.reshape(cases, time_local, pts_count, freq_count, pts_local)]
    dot_general x2, matrix products: 45.1 us -> 31.1 us  [the longest x1 19.7 us: local(): jnp.dot(weighted, full, precision=lax.Precision.HIGH, preferred_element_t...]
    mul x1, other arithmetic: 9.49 us -> 2.17 us  [make_table(): jnp.cos(angle) * scale]
  transfers between devices with their start and end apart: 4 -> 4, of which waited for: 3 -> 3; matrix products, arithmetic and copies ran while one was open for 6% -> 20% of each run, Pallas kernels for 0% -> 0%
where the time goes in v1:
time: 490 us; the launch traced here: 489 us
  waiting for transfers between devices  355 us (72%)
  local copies, waits for them, and re-layouts  57.1 us (12%)
  matrix products  31.1 us (6%)
  other arithmetic  28.5 us (6%)
  between operations  13.1 us (3%)
  starting transfers between devices  5.12 us (1%)
    reduce_scatter x1, waiting for transfers between devices, local(): lax.psum_scatter(spectrum, 'freq', scatter_dimension=2, tiled=True)  145 us
    reduce_scatter x1, waiting for transfers between devices, local(): lax.psum_scatter(partial_value, 'pts', scatter_dimension=3, tiled=True)  117 us
    all_to_all x1, waiting for transfers between devices, local(): lax.all_to_all(histories, 'pts', split_axis=2, concat_axis=1, tiled=True)  92.3 us
    unnamed x5, local copies, waits for them, and re-layouts  43.8 us
    all_to_all x1, other arithmetic, local(): lax.all_to_all(histories, 'pts', split_axis=2, concat_axis=1, tiled=True)  26.2 us
    dot_general x1, matrix products, local(): jnp.dot(weighted, full, precision=lax.Precision.HIGH, preferred_element_t...  19.7 us
    all_to_all x2, local copies, waits for them, and re-layouts, local(): lax.all_to_all(histories, 'pts', split_axis=2, concat_axis=1, tiled=True)  13.2 us
    dot_general x1, matrix products, local(): jnp.einsum('stp,tk->skp', series, table, precision=lax.Precision.HIGH)  11.4 us
  transfers between devices with their start and end apart: 4, of which 3 were waited for; matrix products, arithmetic and copies ran while one was open for 20% of the time, Pallas kernels for 0%

profile of v1, /device:TPU:0, one launch (start us, length us, event | category | flops | bytes accessed | tf_op | source)
XLA Modules:
  0.0 489.4 jit_solution(15101068036198139112)
XLA Ops:
  6.5 0.0 all-gather.2.cloned.1.call-start
  6.5 0.7 all-gather.2.cloned.1.call-update
  7.3 12.3 %copy.5 = f32[8,64,4096]{1,0,2:T(8,128)} copy(f32[8,64,4096]{2,1,0:T(8,128)} %param.3) | data formatting | bytes 16777216 | tf_op args[0]
  19.6 15.9 %reshape.27 = f32[8,1,262144]{2,1,0:T(1,128)} reshape(f32[4096,8,64]{2,1,0:T(8,128)} %bitcast.19) | data formatting | bytes 16777216
  35.5 5.0 %all-to-all-start = ((f32[8,1,262144]{2,1,0:T(1,128)}), f32[8,1,262144]{2,1,0:T(1,128)}, u32[]{:S(2)}, u32[]{:S(2)}) async-start(f32[8,1,262144]{2,1,0:T(1,128)} %reshape.27), calls=%async_computation | async-start | bytes 16777216 | tf_op jit(solution)/shard_map/all_to_all | solution.py:23
  40.5 0.0 reduce-scatter.3.cloned.1.call-start
  40.6 2.2 cosine_multiply_fusion
  42.8 92.3 %all-to-all-done = f32[8,1,262144]{2,1,0:T(1,128)} async-done(((f32[8,1,262144]{2,1,0:T(1,128)}), f32[8,1,262144]{2,1,0:T(1,128)}, u32[]{:S(2)}, u32[]{:S(2)}) %all-to-all-start) | async-done | bytes 8388640 | tf_op jit(solution)/shard_map/all_to_all | solution.py:23
  135.1 0.5 broadcast.46
  135.6 26.2 %reduce = f32[8,262144]{1,0:T(8,128)} reduce(f32[8,1,262144]{2,1,0:T(1,128)} %all-to-all-done, f32[]{:T(128)} %broadcast.46), dimensions={1}, to_apply=%all_to_all.13.reduce_sub_computation | reduce | bytes 16777220 | tf_op jit(solution)/shard_map/all_to_all | solution.py:23
  161.8 15.6 %reshape.28 = f32[4096,8,64]{2,1,0:T(8,128)} reshape(f32[8,262144]{1,0:T(8,128)} %reduce) | data formatting | bytes 16777216
  177.4 12.7 %copy.6 = f32[8,64,8,512]{3,1,2,0:T(8,128)} copy(f32[8,64,8,512]{1,0,3,2:T(8,128)} %bitcast.18) | data formatting | bytes 16777216 | tf_op jit(solution)/shard_map/all_to_all | solution.py:23
  190.1 11.4 %fusion.3 = f32[512,8,512]{2,0,1:T(8,128)} fusion(f32[8,512,512]{2,1,0:T(8,128)} %bitcast.20, f32[512,256]{0,1:T(8,128)S(1)} %get-tuple-element.6, f32[512,256]{0,1:T(8,128)S(1)} %get-tuple-element.5), kind=kOutput, calls=%fused_computation.4 | convolution fusion | flops 6442713088 | bytes 17825792 | tf_op jit(solution)/shard_map/stp,tk->skp/dot_general | solution.py:27
  201.5 0.0 copy-start
  201.5 0.0 reduce-scatter.3.cloned.1.call-update
  201.5 0.0 reduce-scatter.5.cloned.1.call-start
  201.6 0.0 all-gather.2.cloned.1.call-done
  201.6 144.8 %reduce-scatter.3.cloned.1.call-done = f32[8,2,64,512]{3,2,1,0:T(8,128)} async-done(((f32[8,2,256,512]{3,2,1,0:T(8,128)}), f32[8,2,64,512]{3,2,1,0:T(8,128)}) %reduce-scatter.3.cloned.1.call-update) | async-done | bytes 2097168 | tf_op jit(solution)/shard_map/reduce_scatter | solution.py:29
  346.4 0.0 copy-done
  346.4 19.7 %fusion = f32[8,2,64,4096]{3,2,1,0:T(8,128)} fusion(f32[512,4096]{1,0:T(8,128)} %all-gather.2.cloned.1.call-done, f32[8,2,64,512]{3,2,1,0:T(8,128)} %reduce-scatter.3.cloned.1.call-done, f32[512]{0:T(512)S(1)} %copy-done), kind=kOutput, calls=%fused_computation | convolution fusion | flops 12885426176 | bytes 27265024 | tf_op jit(solution)/shard_map/dot_general | solution.py:34
  366.1 0.0 reduce-scatter.5.cloned.1.call-update
  366.1 116.8 %reduce-scatter.5.cloned.1.call-done = f32[8,2,64,512]{3,2,1,0:T(8,128)} async-done(((f32[8,2,64,4096]{3,2,1,0:T(8,128)}), f32[8,2,64,512]{3,2,1,0:T(8,128)}) %reduce-scatter.5.cloned.1.call-update) | async-done | bytes 2097168 | tf_op jit(solution)/shard_map/reduce_scatter | solution.py:38
  (3 shorter events, 0.1 us)
Async XLA Ops:
  6.5 195.1 %all-gather.2.cloned.1.call-start = ((), (), s32[]{:S(2)}) async-start(), calls=%async_computation.4 | async-start | bytes 10485760 | tf_op jit(solution)/shard_map/all_gather | solution.py:33
  35.5 99.6 %all-to-all-start = ((f32[8,1,262144]{2,1,0:T(1,128)}), f32[8,1,262144]{2,1,0:T(1,128)}, u32[]{:S(2)}, u32[]{:S(2)}) async-start(f32[8,1,262144]{2,1,0:T(1,128)} %reshape.27), calls=%async_computation | async-start | bytes 16777216 | tf_op jit(solution)/shard_map/all_to_all | solution.py:23
  40.5 305.9 %reduce-scatter.3.cloned.1.call-start = ((), (), s32[]{:S(2)}) async-start(), calls=%async_computation.3 | async-start | bytes 10485760 | tf_op jit(solution)/shard_map/reduce_scatter | solution.py:29
  201.5 144.9 %copy-start = (f32[512]{0:T(512)S(1)}, f32[512]{0:T(512)}, u32[]{:S(2)}) copy-start(f32[512]{0:T(512)} %param.4) | copy-start | bytes 6148
  201.5 281.3 %reduce-scatter.5.cloned.1.call-start = ((), (), s32[]{:S(2)}) async-start(), calls=%async_computation.5 | async-start | bytes 18874368 | tf_op jit(solution)/shard_map/reduce_scatter | solution.py:38
Sparse Core Ops, SparseCore 0:
  8.9 152.3 all-gather.1
  201.7 144.7 reduce-scatter.2
  366.2 116.5 reduce-scatter.4

commit v2 on v1

v2 whole, which is shorter than its diff:
```python
import functools

import jax
import jax.numpy as jnp
from jax import lax
from jax.experimental import pallas as pl
from jax.experimental.pallas import tpu as pltpu
from jax.sharding import PartitionSpec as P

F = 256
AHEAD = 4
LAG = 2
GROUP = 2
MESH = pl.DeviceIdType.MESH


def make_table(times, total, bins, blocks):
    freqs = jnp.arange(1, bins + 1, dtype=jnp.int32)
    phase_int = freqs[:, None] * times[None, :] % total
    angle = 2.0 * jnp.pi / total * phase_int.astype(jnp.float32)
    window = 0.5 - 0.5 * jnp.cos(2.0 * jnp.pi / total * times.astype(jnp.float32))
    scale = (window / jnp.sqrt(jnp.float32(total)))[None, :]
    cos = (jnp.cos(angle) * scale).reshape(blocks, 1, bins // blocks, -1)
    sin = (-jnp.sin(angle) * scale).reshape(blocks, 1, bins // blocks, -1)
    return jnp.concatenate([cos, sin], axis=1).reshape(2 * bins, -1)


def split(x):
    high = x.astype(jnp.bfloat16)
    return high, (x - high.astype(jnp.float32)).astype(jnp.bfloat16)


def dot3(a, b):
    ah, al = a
    bh, bl = b
    dot = functools.partial(jnp.dot, preferred_element_type=jnp.float32)
    return dot(ah, bh) + (dot(ah, bl) + dot(al, bh))


def kernel(
    nf, np_, hist, table, weight, basis, out,
    h2, bas, rs, spec, wf, th, tl_, wh, wl, cown, csend, pland, fland,
    h_send, h_recv, h_own, b_send_r, b_send_l, b_recv, b_own,
    r_send, r_recv, p_send, p_recv, f_send, f_recv,
):
    cases, time_local, _ = hist.shape
    points = h2.shape[2]
    rows = rs.shape[2]
    per = np_ // nf
    ho = bas.shape[2]
    chips = np_ // 2
    me = lax.axis_index("freq")
    p = lax.axis_index("pts")
    core = lax.rem(p, 2)
    chip = lax.div(p, 2)
    right, left = jnp.minimum(me + 1, nf - 1), jnp.maximum(me - 1, 0)
    has_r, has_l = me < nf - 1, me > 0

    barrier = pltpu.get_barrier_semaphore()
    for d in range(1, np_):
        pl.semaphore_signal(barrier, inc=1, device_id={"pts": lax.rem(p + d, np_)}, device_id_type=MESH)

    @pl.when(has_r)
    def _():
        pl.semaphore_signal(barrier, inc=1, device_id={"freq": right}, device_id_type=MESH)

    @pl.when(has_l)
    def _():
        pl.semaphore_signal(barrier, inc=1, device_id={"freq": left}, device_id_type=MESH)

    inner = jnp.logical_and(has_l, has_r)

    @pl.when(inner)
    def _():
        pl.semaphore_wait(barrier, np_ + 1)

    @pl.when(jnp.logical_not(inner))
    def _():
        pl.semaphore_wait(barrier, np_)

    def b_copy(q, src, to, sems):
        return pltpu.make_async_remote_copy(
            src_ref=src, dst_ref=bas.at[q], send_sem=sems.at[q], recv_sem=b_recv.at[q],
            device_id={"freq": to}, device_id_type=MESH,
        )

    for u in range(per):
        q = me * per + u
        src = basis.at[:, u * ho:(u + 1) * ho]

        @pl.when(has_r)
        def _():
            b_copy(q, src, right, b_send_r).start()

        @pl.when(has_l)
        def _():
            b_copy(q, src, left, b_send_l).start()

        pltpu.make_async_copy(src, bas.at[q], b_own.at[u]).start()

    def b_forward(hop, u):
        @pl.when(me - hop >= 0)
        def _():
            q = (me - hop) * per + u
            copy = b_copy(q, bas.at[q], right, b_send_r)
            copy.wait_recv()

            @pl.when(has_r)
            def _():
                copy.start()

        @pl.when(me + hop <= nf - 1)
        def _():
            q = (me + hop) * per + u
            copy = b_copy(q, bas.at[q], left, b_send_l)
            copy.wait_recv()

            @pl.when(has_l)
            def _():
                copy.start()

    def h_copy(s, q, slot):
        return pltpu.make_async_remote_copy(
            src_ref=hist.at[s, :, pl.ds(pl.multiple_of(q * points, 128), points)],
            dst_ref=h2.at[s, pl.ds(pl.multiple_of(slot * time_local, 8), time_local), :],
            send_sem=h_send.at[s, q], recv_sem=h_recv.at[s, slot],
            device_id={"pts": q}, device_id_type=MESH,
        )

    def h_local(s):
        return pltpu.make_async_copy(
            hist.at[s, :, pl.ds(pl.multiple_of(p * points, 128), points)],
            h2.at[s, pl.ds(pl.multiple_of(p * time_local, 8), time_local), :],
            h_own.at[s],
        )

    def h_start(s):
        for d in range(1, np_):
            h_copy(s, lax.rem(p + d, np_), p).start()
        h_local(s).start()

    for s in range(min(AHEAD, cases)):
        h_start(s)

    high, low = split(table[...])
    th[...] = high
    tl_[...] = low

    def r_copy(s, g, dst, to):
        return pltpu.make_async_remote_copy(
            src_ref=rs.at[s, g], dst_ref=rs.at[s, dst], send_sem=r_send.at[s, g], recv_sem=r_recv.at[s, dst],
            device_id={"freq": to}, device_id_type=MESH,
        )

    def own(g):
        return spec[pl.ds(pl.multiple_of(g * rows, 8), rows), :]

    hops = [(h, u) for h in range(1, nf - 1) for u in range(per)]
    steps = [1 + n * (cases - 1) // max(len(hops), 1) for n in range(len(hops))]

    def transform(i, carry):
        @pl.when(i + AHEAD < cases)
        def _():
            h_start(i + AHEAD)

        @pl.when(i < cases)
        def _():
            for d in range(1, np_):
                q = lax.rem(p + d, np_)
                h_copy(i, q, q).wait_recv()
            h_local(i).wait()
            spec[...] = dot3((th[...], tl_[...]), split(h2[i]))
            for d in range(nf - 1, 0, -1):
                @pl.when(me + d <= nf - 1)
                def _():
                    g = me + d
                    copy = r_copy(i, g, g, right)

                    @pl.when(has_l)
                    def _():
                        copy.wait_recv()
                        rs[i, g] = rs[i, g] + own(g)

                    @pl.when(jnp.logical_not(has_l))
                    def _():
                        rs[i, g] = own(g)

                    copy.start()

                @pl.when(me - d >= 0)
                def _():
                    g = me - d

                    @pl.when(has_r)
                    def _():
                        r_copy(i, g, g, left).wait_recv()
                        rs[i, g] = rs[i, g] + own(g)

                    @pl.when(jnp.logical_not(has_r))
                    def _():
                        rs[i, g] = own(g)

                    r_copy(i, g, nf if d == 1 else g, left).start()

            wf[lax.rem(i, LAG + 1)] = own(me)

        for (hop, u), step in zip(hops, steps):
            @pl.when(i == step)
            def _():
                b_forward(hop, u)

        @pl.when(i >= LAG)
        def _():
            j = i - LAG
            slot = lax.rem(j, LAG + 1)

            @pl.when(has_l)
            def _():
                r_copy(j, me, me, right).wait_recv()
                wf[slot] = wf[slot] + rs[j, me]

            @pl.when(has_r)
            def _():
                r_copy(j, nf, nf, left).wait_recv()
                wf[slot] = wf[slot] + rs[j, nf]

            high, low = split(wf[slot] * weight[...])
            at = pl.ds(pl.multiple_of(j * rows, 16), rows)
            wh[at, :] = high
            wl[at, :] = low

        return carry

    lax.fori_loop(0, cases + LAG, transform, 0)

    for u in range(per):
        b_forward(nf - 1, u)
        q = me * per + u
        pltpu.make_async_copy(basis.at[:, u * ho:(u + 1) * ho], bas.at[q], b_own.at[u]).wait()

    groups, tall = pland.shape[0], pland.shape[2]

    def p_copy(j, slot):
        return pltpu.make_async_remote_copy(
            src_ref=csend.at[slot], dst_ref=pland.at[j], send_sem=p_send.at[slot], recv_sem=p_recv.at[j],
            device_id={"pts": chip * 2 + 1 - core}, device_id_type=MESH,
        )

    def f_copy(j, c, slot):
        return pltpu.make_async_remote_copy(
            src_ref=pland.at[j, c], dst_ref=fland.at[j, slot], send_sem=f_send.at[j, c], recv_sem=f_recv.at[j, slot],
            device_id={"pts": c * 2 + core}, device_id_type=MESH,
        )

    def fit(i, carry):
        @pl.when(i < groups)
        def _():
            slot = lax.rem(i, 2)
            at = pl.ds(pl.multiple_of(i * tall, 16), tall)

            @pl.when(i >= 2)
            def _():
                p_copy(i - 2, slot).wait_send()

            def send_part(c, carry):
                csend[slot, c] = dot3((wh[at, :], wl[at, :]), split(bas[c * 2 + 1 - core]))
                return carry

            lax.fori_loop(0, chips, send_part, 0)
            p_copy(i, slot).start()

            def own_part(c, carry):
                cown[c] = dot3((wh[at, :], wl[at, :]), split(bas[c * 2 + core]))
                return carry

            lax.fori_loop(0, chips, own_part, 0)

        @pl.when(i < groups)
        def _():
            p_copy(i, lax.rem(i, 2)).wait_recv()
            pland[i, chip] = pland[i, chip] + cown[chip]
            for d in range(1, chips):
                c = lax.rem(chip + d, chips)
                pland[i, c] = pland[i, c] + cown[c]
                f_copy(i, c, chip).start()

        @pl.when(i >= 1)
        def _():
            j = i - 1
            total = pland[j, chip]
            for d in range(1, chips):
                c = lax.rem(chip + d, chips)
                f_copy(j, c, c).wait_recv()
                total = total + fland[j, c]
            out[pl.ds(pl.multiple_of(j * tall, 8), tall), :] = total

        return carry

    lax.fori_loop(0, groups + 1, fit, 0)

    def drain(s, carry):
        for d in range(1, np_):
            h_copy(s, lax.rem(p + d, np_), p).wait_send()
        for d in range(1, nf):
            @pl.when(me + d <= nf - 1)
            def _():
                r_copy(s, me + d, me + d, right).wait_send()

            @pl.when(me - d >= 0)
            def _():
                r_copy(s, me - d, me - d, left).wait_send()
        return carry

    lax.fori_loop(0, cases, drain, 0)
    for q in range(np_):
        @pl.when(jnp.logical_and(q // per <= me, has_r))
        def _():
            b_copy(q, bas.at[q], right, b_send_r).wait_send()

        @pl.when(jnp.logical_and(q // per >= me, has_l))
        def _():
            b_copy(q, bas.at[q], left, b_send_l).wait_send()

    for j in range(max(groups - 2, 0), groups):
        p_copy(j, j % 2).wait_send()
    for j in range(groups):
        for d in range(1, chips):
            f_copy(j, lax.rem(chip + d, chips), chip).wait_send()


def local(histories, point_weight, basis):
    nf = lax.axis_size("freq")
    np_ = lax.axis_size("pts")
    cases, time_local, all_points = histories.shape
    points = all_points // np_
    plane_time = time_local * np_
    rows = 2 * F // nf
    ho = basis.shape[1] * nf // np_
    chips = np_ // 2
    tall = GROUP * rows
    groups = cases // GROUP
    times = lax.axis_index("freq") * plane_time + jnp.arange(plane_time, dtype=jnp.int32)
    table = make_table(times, plane_time * nf, F, nf)
    f32, bf16 = jnp.float32, jnp.bfloat16
    hbm = pl.BlockSpec(memory_space=pl.ANY)
    vmem = pl.BlockSpec(memory_space=pltpu.VMEM)
    dma = pltpu.SemaphoreType.DMA
    coeffs = pl.pallas_call(
        functools.partial(kernel, nf, np_),
        out_shape=jax.ShapeDtypeStruct((cases * rows, ho), f32),
        in_specs=[hbm, vmem, vmem, hbm],
        out_specs=vmem,
        scratch_shapes=[
            pltpu.VMEM((cases, plane_time, points), f32),
            pltpu.VMEM((np_, points, ho), f32),
            pltpu.VMEM((cases, nf + 1, rows, points), f32),
            pltpu.VMEM((2 * F, points), f32),
            pltpu.VMEM((LAG + 1, rows, points), f32),
            pltpu.VMEM((2 * F, plane_time), bf16),
            pltpu.VMEM((2 * F, plane_time), bf16),
            pltpu.VMEM((cases * rows, points), bf16),
            pltpu.VMEM((cases * rows, points), bf16),
            pltpu.VMEM((chips, tall, ho), f32),
            pltpu.VMEM((2, chips, tall, ho), f32),
            pltpu.VMEM((groups, chips, tall, ho), f32),
            pltpu.VMEM((groups, chips, tall, ho), f32),
            dma((cases, np_)), dma((cases, np_)), dma((cases,)),
            dma((np_,)), dma((np_,)), dma((np_,)), dma((basis.shape[1] // ho,)),
            dma((cases, nf)), dma((cases, nf + 1)),
            dma((2,)), dma((groups,)),
            dma((groups, chips)), dma((groups, chips)),
        ],
        compiler_params=pltpu.CompilerParams(
            collective_id=0, has_side_effects=True, vmem_limit_bytes=60 * 1024 * 1024
        ),
    )(histories, table, point_weight.reshape(1, -1), basis)
    return coeffs.reshape(cases, 2, rows // 2, ho)


def solution(mesh):
    return jax.shard_map(
        local,
        mesh=mesh,
        in_specs=(P(None, ("freq", "pts"), None), P("pts"), P("pts", "freq")),
        out_specs=P(None, None, "freq", "pts"),
        check_vma=False,
    )
```

time: 490 us -> 336 us (0.69)
  waiting for transfers between devices: 355 us -> 0 us
  Pallas kernels: 0 us -> 329 us
  local copies, waits for them, and re-layouts: 57.1 us -> 3.14 us
  matrix products: 31.1 us -> 0 us
  other arithmetic: 28.5 us -> 3.27 us
  between operations: 13.1 us -> 0.03 us
  starting transfers between devices: 5.12 us -> 0 us
    pallas_call x0 -> x1, Pallas kernels: none -> 329 us  [local(): pl.pallas_call(functools.partial(kernel, nf, np_), out_shape=jax.ShapeDty...]
    reduce_scatter x2 -> x0, waiting for transfers between devices: 262 us -> none  [the longest x1 145 us: local(): lax.psum_scatter(spectrum, 'freq', scatter_dimension=2, tiled=True)]
    all_to_all x1 -> x0, waiting for transfers between devices: 92.3 us -> none  [local(): lax.all_to_all(histories, 'pts', split_axis=2, concat_axis=1, tiled=True)]
    unnamed x5 -> x1, local copies, waits for them, and re-layouts: 43.8 us -> 3.14 us
    dot_general x2 -> x0, matrix products: 31.1 us -> none  [the longest x1 19.7 us: local(): jnp.dot(weighted, full, precision=lax.Precision.HIGH, preferred_element_t...]
    all_to_all x1 -> x0, other arithmetic: 26.2 us -> none  [local(): lax.all_to_all(histories, 'pts', split_axis=2, concat_axis=1, tiled=True)]
    all_to_all x2 -> x0, local copies, waits for them, and re-layouts: 13.2 us -> none  [local(): lax.all_to_all(histories, 'pts', split_axis=2, concat_axis=1, tiled=True)]
    all_to_all x1 -> x0, starting transfers between devices: 5.04 us -> none  [local(): lax.all_to_all(histories, 'pts', split_axis=2, concat_axis=1, tiled=True)]
  transfers between devices with their start and end apart: 4 -> 0, of which waited for: 3 -> 0; matrix products, arithmetic and copies ran while one was open for 20% -> 0% of each run, Pallas kernels for 0% -> 0%
where the time goes in v2:
time: 336 us
  Pallas kernels  329 us (98%)
    pallas_call x1, Pallas kernels, local(): pl.pallas_call(functools.partial(kernel, nf, np_), out_shape=jax.ShapeDty...  329 us

profile of v2, /device:TPU:0, one launch (start us, length us, event | category | flops | bytes accessed | tf_op | source)
XLA Modules:
  0.0 335.6 jit_solution(14695480338663319358)
XLA Ops:
  0.1 2.2 cosine_multiply_fusion
  2.2 1.0 pad_maximum_fusion
  3.3 329.1 %shard_map.37 = f32[1024,512]{1,0:T(8,128)} custom-call(f32[8,64,4096]{2,1,0:T(8,128)} %hist.1, f32[512,512]{1,0:T(8,128)} %bitcast.4, f32[1,512]{1,0:T(1,128)} %bitcast.5, f32[512,1024]{1,0:T(8,128)} %basis.1), custom_call_target="tpu_custom_call" | custom-call | tf_op jit(solution)/shard_map/pallas_call | solution.py:348
  332.4 3.1 copy.5
  (3 shorter events, 0.1 us)

commit v3 on v2

--- a/solution.py
+++ b/solution.py
@@ -10,6 +10,12 @@
 F = 256
 AHEAD = 4
 LAG = 2
+CH = 2
+FIRST = 4
+OWN = 4
+RATE = 0.5
+HOP = 1.0
+BASE = 0.0
 GROUP = 2
 MESH = pl.DeviceIdType.MESH
 
@@ -41,7 +47,7 @@
     nf, np_, hist, table, weight, basis, out,
     h2, bas, rs, spec, wf, th, tl_, wh, wl, cown, csend, pland, fland,
     h_send, h_recv, h_own, b_send_r, b_send_l, b_recv, b_own,
-    r_send, r_recv, p_send, p_recv, f_send, f_recv,
+    r_send, r_recv, p_send, p_recv, f_send, f_recv, o_sem,
 ):
     cases, time_local, _ = hist.shape
     points = h2.shape[2]
@@ -78,31 +84,40 @@
     def _():
         pl.semaphore_wait(barrier, np_)
 
-    def b_copy(q, src, to, sems):
+    part = points // CH
+    chunks = per * CH
+
+    def b_copy(g, n, to, sems, src=None):
+        q = g * per + n // CH
+        dst = bas.at[q, pl.ds(n % CH * part, part), :]
         return pltpu.make_async_remote_copy(
-            src_ref=src, dst_ref=bas.at[q], send_sem=sems.at[q], recv_sem=b_recv.at[q],
+            src_ref=dst if src is None else src, dst_ref=dst,
+            send_sem=sems.at[g, n], recv_sem=b_recv.at[g, n],
             device_id={"freq": to}, device_id_type=MESH,
         )
 
-    for u in range(per):
-        q = me * per + u
-        src = basis.at[:, u * ho:(u + 1) * ho]
-
+    def b_source(n):
+        u = n // CH
+        return basis.at[pl.ds(n % CH * part, part), u * ho:(u + 1) * ho]
+
+    def b_local(n):
+        return pltpu.make_async_copy(
+            b_source(n), bas.at[me * per + n // CH, pl.ds(n % CH * part, part), :], b_own.at[n]
+        )
+
+    def b_start(n):
         @pl.when(has_r)
         def _():
-            b_copy(q, src, right, b_send_r).start()
+            b_copy(me, n, right, b_send_r, b_source(n)).start()
 
         @pl.when(has_l)
         def _():
-            b_copy(q, src, left, b_send_l).start()
-
-        pltpu.make_async_copy(src, bas.at[q], b_own.at[u]).start()
-
-    def b_forward(hop, u):
+            b_copy(me, n, left, b_send_l, b_source(n)).start()
+
+    def b_forward(hop, n):
         @pl.when(me - hop >= 0)
         def _():
-            q = (me - hop) * per + u
-            copy = b_copy(q, bas.at[q], right, b_send_r)
+            copy = b_copy(me - hop, n, right, b_send_r)
             copy.wait_recv()
 
             @pl.when(has_r)
@@ -111,13 +126,23 @@
 
         @pl.when(me + hop <= nf - 1)
         def _():
-            q = (me + hop) * per + u
-            copy = b_copy(q, bas.at[q], left, b_send_l)
+            copy = b_copy(me + hop, n, left, b_send_l)
             copy.wait_recv()
 
             @pl.when(has_l)
             def _():
                 copy.start()
+
+    first = FIRST
+    plan = {}
+    for n in range(chunks):
+        if n >= OWN:
+            plan.setdefault(int((n - OWN) * RATE), []).append((0, n))
+        for hop in range(1, nf - 1):
+            plan.setdefault(min(int(BASE + n * RATE + hop * HOP), first), []).append((hop, n))
+    for n in range(chunks):
+        if n < OWN:
+            b_start(n)
 
     def h_copy(s, q, slot):
         return pltpu.make_async_remote_copy(
@@ -155,10 +180,16 @@
     def own(g):
         return spec[pl.ds(pl.multiple_of(g * rows, 8), rows), :]
 
-    hops = [(h, u) for h in range(1, nf - 1) for u in range(per)]
-    steps = [1 + n * (cases - 1) // max(len(hops), 1) for n in range(len(hops))]
-
-    def transform(i, carry):
+    def transform(i):
+        for step in sorted(plan):
+            @pl.when(i == step)
+            def _():
+                for hop, n in plan[step]:
+                    if hop:
+                        b_forward(hop, n)
+                    else:
+                        b_start(n)
+
         @pl.when(i + AHEAD < cases)
         def _():
             h_start(i + AHEAD)
@@ -204,12 +235,7 @@
 
             wf[lax.rem(i, LAG + 1)] = own(me)
 
-        for (hop, u), step in zip(hops, steps):
-            @pl.when(i == step)
-            def _():
-                b_forward(hop, u)
-
-        @pl.when(i >= LAG)
+        @pl.when(jnp.logical_and(i >= LAG, i < cases + LAG))
         def _():
             j = i - LAG
             slot = lax.rem(j, LAG + 1)
@@ -229,20 +255,12 @@
             wh[at, :] = high
             wl[at, :] = low
 
-        return carry
-
-    lax.fori_loop(0, cases + LAG, transform, 0)
-
-    for u in range(per):
-        b_forward(nf - 1, u)
-        q = me * per + u
-        pltpu.make_async_copy(basis.at[:, u * ho:(u + 1) * ho], bas.at[q], b_own.at[u]).wait()
-
     groups, tall = pland.shape[0], pland.shape[2]
 
-    def p_copy(j, slot):
+    def p_copy(j, c):
         return pltpu.make_async_remote_copy(
-            src_ref=csend.at[slot], dst_ref=pland.at[j], send_sem=p_send.at[slot], recv_sem=p_recv.at[j],
+            src_ref=csend.at[j % 2, c], dst_ref=pland.at[j, c],
+            send_sem=p_send.at[j % 2, c], recv_sem=p_recv.at[j, c],
             device_id={"pts": chip * 2 + 1 - core}, device_id_type=MESH,
         )
 
@@ -252,51 +270,72 @@
             device_id={"pts": c * 2 + core}, device_id_type=MESH,
         )
 
-    def fit(i, carry):
-        @pl.when(i < groups)
-        def _():
-            slot = lax.rem(i, 2)
-            at = pl.ds(pl.multiple_of(i * tall, 16), tall)
-
-            @pl.when(i >= 2)
-            def _():
-                p_copy(i - 2, slot).wait_send()
-
-            def send_part(c, carry):
-                csend[slot, c] = dot3((wh[at, :], wl[at, :]), split(bas[c * 2 + 1 - core]))
-                return carry
-
-            lax.fori_loop(0, chips, send_part, 0)
-            p_copy(i, slot).start()
-
-            def own_part(c, carry):
-                cown[c] = dot3((wh[at, :], wl[at, :]), split(bas[c * 2 + core]))
-                return carry
-
-            lax.fori_loop(0, chips, own_part, 0)
-
-        @pl.when(i < groups)
-        def _():
-            p_copy(i, lax.rem(i, 2)).wait_recv()
-            pland[i, chip] = pland[i, chip] + cown[chip]
-            for d in range(1, chips):
-                c = lax.rem(chip + d, chips)
-                pland[i, c] = pland[i, c] + cown[c]
-                f_copy(i, c, chip).start()
-
-        @pl.when(i >= 1)
-        def _():
-            j = i - 1
-            total = pland[j, chip]
-            for d in range(1, chips):
-                c = lax.rem(chip + d, chips)
-                f_copy(j, c, c).wait_recv()
-                total = total + fland[j, c]
-            out[pl.ds(pl.multiple_of(j * tall, 8), tall), :] = total
+    def o_copy(j):
+        return pltpu.make_async_copy(
+            pland.at[j, chip], out.at[pl.ds(pl.multiple_of(j * tall, 8), tall), :], o_sem.at[j]
+        )
+
+    def fit(j):
+        at = pl.ds(j * tall, tall)
+
+        def pass_on(d):
+            c = lax.rem(chip + d, chips)
+            p_copy(j, c).wait_recv()
+            pland[j, c] = pland[j, c] + cown[c]
+
+            @pl.when(d < chips)
+            def _():
+                f_copy(j, c, chip).start()
+
+        def part(d, carry):
+            c = lax.rem(chip + d, chips)
+            if j >= 2:
+                p_copy(j - 2, c).wait_send()
+            csend[j % 2, c] = dot3((wh[at, :], wl[at, :]), split(bas[c * 2 + 1 - core]))
+            p_copy(j, c).start()
+            cown[c] = dot3((wh[at, :], wl[at, :]), split(bas[c * 2 + core]))
+
+            @pl.when(d > 1)
+            def _():
+                pass_on(d - 1)
+
+            return carry
+
+        lax.fori_loop(1, chips + 1, part, 0)
+        pass_on(chips)
+
+    def finish(j):
+        total = pland[j, chip]
+        for d in range(1, chips):
+            c = lax.rem(chip + d, chips)
+            f_copy(j, c, c).wait_recv()
+            total = total + fland[j, c]
+        pland[j, chip] = total
+        o_copy(j).start()
+
+    fits = [max(first + g, GROUP * (g + 1) - 1 + LAG) for g in range(groups)]
+
+    def step(i, carry):
+        transform(i)
+
+        @pl.when(i == first)
+        def _():
+            for n in range(chunks):
+                b_forward(nf - 1, n)
+                b_local(n).wait()
+
+        for g in range(groups):
+            @pl.when(i == fits[g])
+            def _():
+                fit(g)
 
         return carry
 
-    lax.fori_loop(0, groups + 1, fit, 0)
+    for n in range(chunks):
+        b_local(n).start()
+    lax.fori_loop(0, max(cases + LAG, fits[-1] + 1), step, 0)
+    for g in range(groups):
+        finish(g)
 
     def drain(s, carry):
         for d in range(1, np_):
@@ -312,17 +351,22 @@
         return carry
 
     lax.fori_loop(0, cases, drain, 0)
-    for q in range(np_):
-        @pl.when(jnp.logical_and(q // per <= me, has_r))
-        def _():
-            b_copy(q, bas.at[q], right, b_send_r).wait_send()
-
-        @pl.when(jnp.logical_and(q // per >= me, has_l))
-        def _():
-            b_copy(q, bas.at[q], left, b_send_l).wait_send()
-
+    for g in range(nf):
+        @pl.when(jnp.logical_and(g <= me, has_r))
+        def _():
+            for n in range(chunks):
+                b_copy(g, n, right, b_send_r).wait_send()
+
+        @pl.when(jnp.logical_and(g >= me, has_l))
+        def _():
+            for n in range(chunks):
+                b_copy(g, n, left, b_send_l).wait_send()
+
+    for j in range(groups):
+        o_copy(j).wait()
     for j in range(max(groups - 2, 0), groups):
-        p_copy(j, j % 2).wait_send()
+        for c in range(chips):
+            p_copy(j, c).wait_send()
     for j in range(groups):
         for d in range(1, chips):
             f_copy(j, lax.rem(chip + d, chips), chip).wait_send()
@@ -336,6 +380,7 @@
     plane_time = time_local * np_
     rows = 2 * F // nf
     ho = basis.shape[1] * nf // np_
+    chunks = np_ // nf * CH
     chips = np_ // 2
     tall = GROUP * rows
     groups = cases // GROUP
@@ -349,7 +394,7 @@
         functools.partial(kernel, nf, np_),
         out_shape=jax.ShapeDtypeStruct((cases * rows, ho), f32),
         in_specs=[hbm, vmem, vmem, hbm],
-        out_specs=vmem,
+        out_specs=hbm,
         scratch_shapes=[
             pltpu.VMEM((cases, plane_time, points), f32),
             pltpu.VMEM((np_, points, ho), f32),
@@ -365,10 +410,10 @@
             pltpu.VMEM((groups, chips, tall, ho), f32),
             pltpu.VMEM((groups, chips, tall, ho), f32),
             dma((cases, np_)), dma((cases, np_)), dma((cases,)),
-            dma((np_,)), dma((np_,)), dma((np_,)), dma((basis.shape[1] // ho,)),
+            dma((nf, chunks)), dma((nf, chunks)), dma((nf, chunks)), dma((chunks,)),
             dma((cases, nf)), dma((cases, nf + 1)),
-            dma((2,)), dma((groups,)),
-            dma((groups, chips)), dma((groups, chips)),
+            dma((2, chips)), dma((groups, chips)),
+            dma((groups, chips)), dma((groups, chips)), dma((groups,)),
         ],
         compiler_params=pltpu.CompilerParams(
             collective_id=0, has_side_effects=True, vmem_limit_bytes=60 * 1024 * 1024

time: 336 us -> 296 us (0.88)
  the two profiles are of different devices: /device:TPU:0 before, /device:TPU:18 now
where the time goes in v3:
time: 296 us
  Pallas kernels  290 us (98%)
  other arithmetic  3.27 us (1%)
  local copies, waits for them, and re-layouts  3.14 us (1%)
    pallas_call x1, Pallas kernels, local(): pl.pallas_call(functools.partial(kernel, nf, np_), out_shape=jax.ShapeDty...  290 us

profile of v3, /device:TPU:18, one launch (start us, length us, event | category | flops | bytes accessed | tf_op | source)
XLA Modules:
  0.0 296.2 jit_solution(17325143148092756919)
XLA Ops:
  0.1 2.2 cosine_multiply_fusion
  2.2 1.0 pad_maximum_fusion
  3.3 289.8 %shard_map.37 = f32[1024,512]{1,0:T(8,128)} custom-call(f32[8,64,4096]{2,1,0:T(8,128)} %hist.1, f32[512,512]{1,0:T(8,128)} %bitcast.4, f32[1,512]{1,0:T(1,128)} %bitcast.5, f32[512,1024]{1,0:T(8,128)} %basis.1), custom_call_target="tpu_custom_call" | custom-call | tf_op jit(solution)/shard_map/pallas_call | solution.py:393
  293.1 3.1 %copy.5 = f32[8,2,64,512]{3,2,1,0:T(8,128)} copy(f32[8,2,64,512]{3,2,1,0:T(8,128)} %bitcast.3) | data formatting | bytes 4194304
  (3 shorter events, 0.1 us)
